TPU v7x, 512 devices: a whole 4x8x8 slice. The times are simulated.
512 devices in a mesh: mem: 16 (over y, core), lat: 8 (over x, z_hi), lon: 4 (over z_lo).
Axes of the slice: x: 4, y: 8, z: 8 (z_hi: 2, z_lo: 4; z = z_hi * 4 + z_lo), core: 2. Of those that a mesh axis runs over, the one named last changes fastest.
Arguments:
- members: bfloat16 [32, 8, 256, 512], P('mem', None, 'lat', 'lon'), may hold values from -6 to 6
- increment: float32 [8, 256, 512], P(None, 'lat', 'lon'), may hold values from -6 to 6
Outputs:
- covariance_product: float32 [8, 256, 512], P(None, 'lat', 'lon')
All inputs are finite; a program needn't handle non-finite values.
Results may differ from a plain program's by a relative error of at most 0.0003.
Values sent between devices are 32-bit elements; how exact they have to be, the bound alone decides.
No kernel may reach another device: no remote copies, remote signals or barrier semaphores. Data moves between devices by JAX's collectives and lax.ppermute only.
A program may use at most 64 MiB of HBM per device.

v0:
```python
import jax
import jax.numpy as jnp
from jax import lax
from jax.sharding import PartitionSpec as P

ITERS = 4
factors = (1, 2, 4)
stiffnesses = (1.0, 2.0, 4.0)
weights = (0.5, 0.3, 0.2)


def with_halo(block, sides, width, periodic):
    for axis, dim in sides:
        count = lax.axis_size(axis)
        forward = [(i, i + 1) for i in range(count - 1)]
        if periodic:
            forward.append((count - 1, 0))
        backward = [(target, source) for source, target in forward]
        low = lax.ppermute(
            lax.slice_in_dim(block, block.shape[dim] - width, None, axis=dim), axis, forward
        )
        high = lax.ppermute(lax.slice_in_dim(block, 0, width, axis=dim), axis, backward)
        block = jnp.concatenate([low, block, high], axis=dim)
    return block


def coarsen(values_now, factor):
    if factor == 1:
        return values_now
    dims_now = values_now.shape
    blocks = values_now.reshape(
        dims_now[:-2] + (dims_now[-2] // factor, factor, dims_now[-1] // factor, factor)
    )
    return jnp.mean(blocks, axis=(-3, -1))


def refine(values_now, factor):
    if factor == 1:
        return values_now
    return jnp.repeat(jnp.repeat(values_now, factor, axis=-2), factor, axis=-1)


def diffuse_single(source, stiffness):
    smoothed = source
    for sweeps in range(ITERS):
        with_rows = with_halo(smoothed, (("lat", 2),), 1, False)
        with_cols = with_halo(smoothed, (("lon", 3),), 1, True)
        beside_all = with_rows[:, :, :-2, :] + with_rows[:, :, 2:, :]
        beside_all = beside_all + with_cols[:, :, :, :-2] + with_cols[:, :, :, 2:]
        smoothed = (source + stiffness * beside_all) / (1.0 + 4.0 * stiffness)
    return smoothed


def body(members, increment):
    member_field = members.astype(jnp.float32)
    product = member_field * increment[None]
    running = jnp.zeros(member_field.shape, jnp.float32)
    for factor, stiffness, weight in zip(factors, stiffnesses, weights):
        source = coarsen(product, factor)
        coarse = diffuse_single(source, stiffness)
        running = running + weight * member_field * refine(coarse, factor)
    partial_value = jnp.sum(running, axis=0)
    member_count = members.shape[0] * lax.axis_size("mem")
    summed = lax.psum(partial_value, "mem")
    return summed / (member_count - 1)


def solution(mesh):
    return jax.shard_map(
        body,
        mesh=mesh,
        in_specs=(P("mem", None, "lat", "lon"), P(None, "lat", "lon")),
        out_specs=P(None, "lat", "lon"),
        check_vma=False,
    )
```

profile of v0, /device:TPU:1, one launch (start us, length us, event | category | flops | bytes accessed | tf_op | source)
XLA Modules:
  0.0 434.9 jit_solution(4924736812012016826)
XLA Ops:
  9.0 4.3 copy.364
  13.3 5.6 %reduce_sum.27 = f32[2,8,16,64]{1,3,2,0:T(8,128)S(1)} reduce(f32[2,8,16,2,64,2]{1,5,4,3,2,0:T(2,128)} %bitcast.6, f32[]{:T(128)} %constant.30.clone.1), dimensions={3,5}, to_apply=%region_0.0 | reduce | flops 49152 | bytes 327684 | tf_op jit(solution)/shard_map/reduce_sum | solution.py:34
  20.1 8.4 %collective-permute-start.19 = (f32[2,8,16,1]{3,2,1,0:T(8,128)}, f32[2,8,16,1]{3,2,1,0:T(8,128)}, u32[]{:S(2)}, u32[]{:S(2)}) collective-permute-start(f32[2,8,16,1]{3,2,1,0:T(8,128)} %get-tuple-element.52), channel_id=1, source_target_pairs={{1,0},{2,1},{3,2},{0,3},{5,4},{6,5},{7,6},{4,7},{9,8},{10,9},{11,1... | collective-permute-start | bytes 3080 | tf_op jit(solution)/shard_map/ppermute | solution.py:22
  38.8 8.6 %collective-permute-start.32 = (f32[2,8,1,32]{1,3,2,0:T(8,128)S(1)}, f32[2,8,1,32]{1,3,2,0:T(8,128)S(1)}, u32[]{:S(2)}, u32[]{:S(2)}) collective-permute-start(f32[2,8,1,32]{1,3,2,0:T(8,128)S(1)} %get-tuple-element.33), channel_id=1, source_target_pairs={{0,4},{4,8},{8,12},{12,16},{16,20},{20,24},{24,28},{1,5},{5,9},{9,... | collective-permute-start | bytes 6152 | tf_op jit(solution)/shard_map/ppermute | solution.py:19
  58.9 9.4 %collective-permute-start.36 = (f32[2,8,1,32]{1,3,2,0:T(8,128)}, f32[2,8,1,32]{1,3,2,0:T(8,128)}, u32[]{:S(2)}, u32[]{:S(2)}) collective-permute-start(f32[2,8,1,32]{1,3,2,0:T(8,128)} %get-tuple-element.29), channel_id=1, source_target_pairs={{0,4},{4,8},{8,12},{12,16},{16,20},{20,24},{24,28},{1,5},{5,9},{9,... | collective-permute-start | bytes 6152 | tf_op jit(solution)/shard_map/ppermute | solution.py:19
  74.6 8.2 %collective-permute-start.16 = (f32[2,8,1,64]{3,2,1,0:T(1,128)}, f32[2,8,1,64]{3,2,1,0:T(1,128)S(1)}, u32[]{:S(2)}, u32[]{:S(2)}) collective-permute-start(f32[2,8,1,64]{3,2,1,0:T(1,128)} %get-tuple-element.49), channel_id=1, source_target_pairs={{0,4},{4,8},{8,12},{12,16},{16,20},{20,24},{24,28},{1,5},{5,9},{9,... | collective-permute-start | bytes 12296 | tf_op jit(solution)/shard_map/ppermute | solution.py:19
  82.9 5.2 %collective-permute-start.3 = (f32[2,8,32,1]{2,1,3,0:T(8,128)}, f32[2,8,32,1]{2,1,3,0:T(8,128)S(1)}, u32[]{:S(2)}, u32[]{:S(2)}) collective-permute-start(f32[2,8,32,1]{2,1,3,0:T(8,128)} %get-tuple-element.20), channel_id=1, source_target_pairs={{1,0},{2,1},{3,2},{0,3},{5,4},{6,5},{7,6},{4,7},{9,8},{10,9},{11,1... | collective-permute-start | bytes 6152 | tf_op jit(solution)/shard_map/ppermute | solution.py:22
  97.8 8.8 %collective-permute-start.40 = (f32[2,8,1,32]{1,3,2,0:T(8,128)S(1)}, f32[2,8,1,32]{1,3,2,0:T(8,128)S(1)}, u32[]{:S(2)}, u32[]{:S(2)}) collective-permute-start(f32[2,8,1,32]{1,3,2,0:T(8,128)S(1)} %get-tuple-element.25), channel_id=1, source_target_pairs={{0,4},{4,8},{8,12},{12,16},{16,20},{20,24},{24,28},{1,5},{5,9},{9,... | collective-permute-start | bytes 6152 | tf_op jit(solution)/shard_map/ppermute | solution.py:19
  106.6 5.2 %collective-permute-start.23 = (f32[2,8,16,1]{3,2,1,0:T(8,128)S(1)}, f32[2,8,16,1]{3,2,1,0:T(8,128)S(1)}, u32[]{:S(2)}, u32[]{:S(2)}) collective-permute-start(f32[2,8,16,1]{3,2,1,0:T(8,128)S(1)} %get-tuple-element.48), channel_id=1, source_target_pairs={{1,0},{2,1},{3,2},{0,3},{5,4},{6,5},{7,6},{4,7},{9,8},{10,9},{11,1... | collective-permute-start | bytes 3080 | tf_op jit(solution)/shard_map/ppermute | solution.py:22
  115.1 8.8 %collective-permute-start.20 = (f32[2,8,1,64]{3,2,1,0:T(1,128)S(1)}, f32[2,8,1,64]{3,2,1,0:T(1,128)S(1)}, u32[]{:S(2)}, u32[]{:S(2)}) collective-permute-start(f32[2,8,1,64]{3,2,1,0:T(1,128)S(1)} %get-tuple-element.45), channel_id=1, source_target_pairs={{0,4},{4,8},{8,12},{12,16},{16,20},{20,24},{24,28},{1,5},{5,9},{9,... | collective-permute-start | bytes 12296 | tf_op jit(solution)/shard_map/ppermute | solution.py:19
  128.6 8.8 %collective-permute-start = (f32[2,8,1,128]{3,1,2,0:T(8,128)S(1)}, f32[2,8,1,128]{3,1,2,0:T(8,128)S(1)}, u32[]{:S(2)}, u32[]{:S(2)}) collective-permute-start(f32[2,8,1,128]{3,1,2,0:T(8,128)S(1)} %copy.348), channel_id=1, source_target_pairs={{0,4},{4,8},{8,12},{12,16},{16,20},{20,24},{24,28},{1,5},{5,9},{9,... | collective-permute-start | bytes 24584 | tf_op jit(solution)/shard_map/ppermute | solution.py:19
  137.4 5.2 %collective-permute-start.47 = (f32[2,8,8,1]{1,3,2,0:T(1,128)}, f32[2,8,8,1]{1,3,2,0:T(1,128)}, u32[]{:S(2)}, u32[]{:S(2)}) collective-permute-start(f32[2,8,8,1]{1,3,2,0:T(1,128)} %get-tuple-element.24), channel_id=1, source_target_pairs={{1,0},{2,1},{3,2},{0,3},{5,4},{6,5},{7,6},{4,7},{9,8},{10,9},{11,1... | collective-permute-start | bytes 1544 | tf_op jit(solution)/shard_map/ppermute | solution.py:22
  149.5 8.8 %collective-permute-start.44 = (f32[2,8,1,32]{1,3,2,0:T(8,128)}, f32[2,8,1,32]{1,3,2,0:T(8,128)S(1)}, u32[]{:S(2)}, u32[]{:S(2)}) collective-permute-start(f32[2,8,1,32]{1,3,2,0:T(8,128)} %get-tuple-element.21), channel_id=1, source_target_pairs={{0,4},{4,8},{8,12},{12,16},{16,20},{20,24},{24,28},{1,5},{5,9},{9,... | collective-permute-start | bytes 6152 | tf_op jit(solution)/shard_map/ppermute | solution.py:19
  158.9 5.3 %collective-permute-start.27 = (f32[2,8,16,1]{3,2,1,0:T(8,128)}, f32[2,8,16,1]{3,2,1,0:T(8,128)}, u32[]{:S(2)}, u32[]{:S(2)}) collective-permute-start(f32[2,8,16,1]{3,2,1,0:T(8,128)} %get-tuple-element.44), channel_id=1, source_target_pairs={{1,0},{2,1},{3,2},{0,3},{5,4},{6,5},{7,6},{4,7},{9,8},{10,9},{11,1... | collective-permute-start | bytes 3080 | tf_op jit(solution)/shard_map/ppermute | solution.py:22
  172.8 9.4 %collective-permute-start.24 = (f32[2,8,1,64]{3,2,1,0:T(1,128)}, f32[2,8,1,64]{3,2,1,0:T(1,128)}, u32[]{:S(2)}, u32[]{:S(2)}) collective-permute-start(f32[2,8,1,64]{3,2,1,0:T(1,128)} %get-tuple-element.41), channel_id=1, source_target_pairs={{0,4},{4,8},{8,12},{12,16},{16,20},{20,24},{24,28},{1,5},{5,9},{9,... | collective-permute-start | bytes 12296 | tf_op jit(solution)/shard_map/ppermute | solution.py:19
  187.8 5.1 %collective-permute-start.7 = (f32[2,8,32,1]{2,1,3,0:T(8,128)}, f32[2,8,32,1]{2,1,3,0:T(8,128)S(1)}, u32[]{:S(2)}, u32[]{:S(2)}) collective-permute-start(f32[2,8,32,1]{2,1,3,0:T(8,128)} %get-tuple-element.16), channel_id=1, source_target_pairs={{1,0},{2,1},{3,2},{0,3},{5,4},{6,5},{7,6},{4,7},{9,8},{10,9},{11,1... | collective-permute-start | bytes 6152 | tf_op jit(solution)/shard_map/ppermute | solution.py:22
  199.3 8.2 %collective-permute-start.4 = (f32[2,8,1,128]{3,1,2,0:T(8,128)}, f32[2,8,1,128]{3,1,2,0:T(8,128)S(1)}, u32[]{:S(2)}, u32[]{:S(2)}) collective-permute-start(f32[2,8,1,128]{3,1,2,0:T(8,128)} %copy.352), channel_id=1, source_target_pairs={{0,4},{4,8},{8,12},{12,16},{16,20},{20,24},{24,28},{1,5},{5,9},{9,... | collective-permute-start | bytes 24584 | tf_op jit(solution)/shard_map/ppermute | solution.py:19
  216.8 5.1 %collective-permute-start.11 = (f32[2,8,32,1]{2,1,3,0:T(8,128)}, f32[2,8,32,1]{2,1,3,0:T(8,128)S(1)}, u32[]{:S(2)}, u32[]{:S(2)}) collective-permute-start(f32[2,8,32,1]{2,1,3,0:T(8,128)} %get-tuple-element.12), channel_id=1, source_target_pairs={{1,0},{2,1},{3,2},{0,3},{5,4},{6,5},{7,6},{4,7},{9,8},{10,9},{11,1... | collective-permute-start | bytes 6152 | tf_op jit(solution)/shard_map/ppermute | solution.py:22
  228.3 8.8 %collective-permute-start.8 = (f32[2,8,1,128]{3,1,2,0:T(8,128)}, f32[2,8,1,128]{3,1,2,0:T(8,128)S(1)}, u32[]{:S(2)}, u32[]{:S(2)}) collective-permute-start(f32[2,8,1,128]{3,1,2,0:T(8,128)} %copy.356), channel_id=1, source_target_pairs={{0,4},{4,8},{8,12},{12,16},{16,20},{20,24},{24,28},{1,5},{5,9},{9,... | collective-permute-start | bytes 24584 | tf_op jit(solution)/shard_map/ppermute | solution.py:19
  237.7 5.2 %collective-permute-start.31 = (f32[2,8,16,1]{3,2,1,0:T(8,128)}, f32[2,8,16,1]{3,2,1,0:T(8,128)}, u32[]{:S(2)}, u32[]{:S(2)}) collective-permute-start(f32[2,8,16,1]{3,2,1,0:T(8,128)} %get-tuple-element.40), channel_id=1, source_target_pairs={{1,0},{2,1},{3,2},{0,3},{5,4},{6,5},{7,6},{4,7},{9,8},{10,9},{11,1... | collective-permute-start | bytes 3080 | tf_op jit(solution)/shard_map/ppermute | solution.py:22
  248.9 9.4 %collective-permute-start.28 = (f32[2,8,1,64]{3,2,1,0:T(1,128)}, f32[2,8,1,64]{3,2,1,0:T(1,128)}, u32[]{:S(2)}, u32[]{:S(2)}) collective-permute-start(f32[2,8,1,64]{3,2,1,0:T(1,128)} %get-tuple-element.37), channel_id=1, source_target_pairs={{0,4},{4,8},{8,12},{12,16},{16,20},{20,24},{24,28},{1,5},{5,9},{9,... | collective-permute-start | bytes 12296 | tf_op jit(solution)/shard_map/ppermute | solution.py:19
  262.7 5.1 %collective-permute-start.15 = (f32[2,8,32,1]{2,1,3,0:T(8,128)}, f32[2,8,32,1]{2,1,3,0:T(8,128)S(1)}, u32[]{:S(2)}, u32[]{:S(2)}) collective-permute-start(f32[2,8,32,1]{2,1,3,0:T(8,128)} %get-tuple-element.8), channel_id=1, source_target_pairs={{1,0},{2,1},{3,2},{0,3},{5,4},{6,5},{7,6},{4,7},{9,8},{10,9},{11,1... | collective-permute-start | bytes 6152 | tf_op jit(solution)/shard_map/ppermute | solution.py:22
  274.2 8.8 %collective-permute-start.12 = (f32[2,8,1,128]{3,1,2,0:T(8,128)}, f32[2,8,1,128]{3,1,2,0:T(8,128)}, u32[]{:S(2)}, u32[]{:S(2)}) collective-permute-start(f32[2,8,1,128]{3,1,2,0:T(8,128)} %copy.360), channel_id=1, source_target_pairs={{0,4},{4,8},{8,12},{12,16},{16,20},{20,24},{24,28},{1,5},{5,9},{9,... | collective-permute-start | bytes 24584 | tf_op jit(solution)/shard_map/ppermute | solution.py:19
  294.7 131.7 %all-reduce.2.cloned.1.call-done = f32[8,32,128]{2,1,0:T(8,128)} async-done(((f32[8,32,128]{2,1,0:T(8,128)}), f32[8,32,128]{2,1,0:T(8,128)}) %all-reduce.2.cloned.1.call-update) | async-done | bytes 131088 | tf_op jit(solution)/shard_map/psum | solution.py:64
  (162 shorter events, 123.2 us)
Async XLA Ops:
  6.5 419.9 %all-reduce.2.cloned.1.call-start = ((), (), s32[]{:S(2)}) async-start(), calls=%async_computation | async-start | bytes 262144 | tf_op jit(solution)/shard_map/psum | solution.py:64
  20.1 69.4 %collective-permute-start.19 = (f32[2,8,16,1]{3,2,1,0:T(8,128)}, f32[2,8,16,1]{3,2,1,0:T(8,128)}, u32[]{:S(2)}, u32[]{:S(2)}) collective-permute-start(f32[2,8,16,1]{3,2,1,0:T(8,128)} %get-tuple-element.52), channel_id=1, source_target_pairs={{1,0},{2,1},{3,2},{0,3},{5,4},{6,5},{7,6},{4,7},{9,8},{10,9},{11,1... | collective-permute-start | bytes 3080 | tf_op jit(solution)/shard_map/ppermute | solution.py:22
  51.7 19.7 %collective-permute-start.39 = (f32[2,8,8,1]{1,3,2,0:T(1,128)}, f32[2,8,8,1]{1,3,2,0:T(1,128)S(1)}, u32[]{:S(2)}, u32[]{:S(2)}) collective-permute-start(f32[2,8,8,1]{1,3,2,0:T(1,128)} %get-tuple-element.32), channel_id=1, source_target_pairs={{1,0},{2,1},{3,2},{0,3},{5,4},{6,5},{7,6},{4,7},{9,8},{10,9},{11,1... | collective-permute-start | bytes 1544 | tf_op jit(solution)/shard_map/ppermute | solution.py:22
  58.9 24.0 %collective-permute-start.36 = (f32[2,8,1,32]{1,3,2,0:T(8,128)}, f32[2,8,1,32]{1,3,2,0:T(8,128)}, u32[]{:S(2)}, u32[]{:S(2)}) collective-permute-start(f32[2,8,1,32]{1,3,2,0:T(8,128)} %get-tuple-element.29), channel_id=1, source_target_pairs={{0,4},{4,8},{8,12},{12,16},{16,20},{20,24},{24,28},{1,5},{5,9},{9,... | collective-permute-start | bytes 6152 | tf_op jit(solution)/shard_map/ppermute | solution.py:19
  82.9 66.6 %collective-permute-start.3 = (f32[2,8,32,1]{2,1,3,0:T(8,128)}, f32[2,8,32,1]{2,1,3,0:T(8,128)S(1)}, u32[]{:S(2)}, u32[]{:S(2)}) collective-permute-start(f32[2,8,32,1]{2,1,3,0:T(8,128)} %get-tuple-element.20), channel_id=1, source_target_pairs={{1,0},{2,1},{3,2},{0,3},{5,4},{6,5},{7,6},{4,7},{9,8},{10,9},{11,1... | collective-permute-start | bytes 6152 | tf_op jit(solution)/shard_map/ppermute | solution.py:22
  106.6 18.7 %collective-permute-start.23 = (f32[2,8,16,1]{3,2,1,0:T(8,128)S(1)}, f32[2,8,16,1]{3,2,1,0:T(8,128)S(1)}, u32[]{:S(2)}, u32[]{:S(2)}) collective-permute-start(f32[2,8,16,1]{3,2,1,0:T(8,128)S(1)} %get-tuple-element.48), channel_id=1, source_target_pairs={{1,0},{2,1},{3,2},{0,3},{5,4},{6,5},{7,6},{4,7},{9,8},{10,9},{11,1... | collective-permute-start | bytes 3080 | tf_op jit(solution)/shard_map/ppermute | solution.py:22
  115.1 22.3 %collective-permute-start.20 = (f32[2,8,1,64]{3,2,1,0:T(1,128)S(1)}, f32[2,8,1,64]{3,2,1,0:T(1,128)S(1)}, u32[]{:S(2)}, u32[]{:S(2)}) collective-permute-start(f32[2,8,1,64]{3,2,1,0:T(1,128)S(1)} %get-tuple-element.45), channel_id=1, source_target_pairs={{0,4},{4,8},{8,12},{12,16},{16,20},{20,24},{24,28},{1,5},{5,9},{9,... | collective-permute-start | bytes 12296 | tf_op jit(solution)/shard_map/ppermute | solution.py:19
  125.3 33.0 %collective-permute-start.2 = (f32[2,8,32,1]{2,1,3,0:T(8,128)}, f32[2,8,32,1]{2,1,3,0:T(8,128)S(1)}, u32[]{:S(2)}, u32[]{:S(2)}) collective-permute-start(f32[2,8,32,1]{2,1,3,0:T(8,128)} %get-tuple-element.19), channel_id=1, source_target_pairs={{0,1},{1,2},{2,3},{3,0},{4,5},{5,6},{6,7},{7,4},{8,9},{9,10},{10,1... | collective-permute-start | bytes 6152 | tf_op jit(solution)/shard_map/ppermute | solution.py:19
  137.4 32.2 %collective-permute-start.47 = (f32[2,8,8,1]{1,3,2,0:T(1,128)}, f32[2,8,8,1]{1,3,2,0:T(1,128)}, u32[]{:S(2)}, u32[]{:S(2)}) collective-permute-start(f32[2,8,8,1]{1,3,2,0:T(1,128)} %get-tuple-element.24), channel_id=1, source_target_pairs={{1,0},{2,1},{3,2},{0,3},{5,4},{6,5},{7,6},{4,7},{9,8},{10,9},{11,1... | collective-permute-start | bytes 1544 | tf_op jit(solution)/shard_map/ppermute | solution.py:22
  143.5 28.0 %collective-permute-start.46 = (f32[2,8,8,1]{1,3,2,0:T(1,128)}, f32[2,8,8,1]{1,3,2,0:T(1,128)}, u32[]{:S(2)}, u32[]{:S(2)}) collective-permute-start(f32[2,8,8,1]{1,3,2,0:T(1,128)} %get-tuple-element.23), channel_id=1, source_target_pairs={{0,1},{1,2},{2,3},{3,0},{4,5},{5,6},{6,7},{7,4},{8,9},{9,10},{10,1... | collective-permute-start | bytes 1544 | tf_op jit(solution)/shard_map/ppermute | solution.py:19
  146.8 26.0 %collective-permute-start.45 = (f32[2,8,1,32]{1,3,2,0:T(8,128)}, f32[2,8,1,32]{1,3,2,0:T(8,128)}, u32[]{:S(2)}, u32[]{:S(2)}) collective-permute-start(f32[2,8,1,32]{1,3,2,0:T(8,128)} %get-tuple-element.22), channel_id=1, source_target_pairs={{4,0},{8,4},{12,8},{16,12},{20,16},{24,20},{28,24},{5,1},{9,5},{13... | collective-permute-start | bytes 6152 | tf_op jit(solution)/shard_map/ppermute | solution.py:22
  149.5 32.7 %collective-permute-start.44 = (f32[2,8,1,32]{1,3,2,0:T(8,128)}, f32[2,8,1,32]{1,3,2,0:T(8,128)S(1)}, u32[]{:S(2)}, u32[]{:S(2)}) collective-permute-start(f32[2,8,1,32]{1,3,2,0:T(8,128)} %get-tuple-element.21), channel_id=1, source_target_pairs={{0,4},{4,8},{8,12},{12,16},{16,20},{20,24},{24,28},{1,5},{5,9},{9,... | collective-permute-start | bytes 6152 | tf_op jit(solution)/shard_map/ppermute | solution.py:19
  158.9 37.2 %collective-permute-start.27 = (f32[2,8,16,1]{3,2,1,0:T(8,128)}, f32[2,8,16,1]{3,2,1,0:T(8,128)}, u32[]{:S(2)}, u32[]{:S(2)}) collective-permute-start(f32[2,8,16,1]{3,2,1,0:T(8,128)} %get-tuple-element.44), channel_id=1, source_target_pairs={{1,0},{2,1},{3,2},{0,3},{5,4},{6,5},{7,6},{4,7},{9,8},{10,9},{11,1... | collective-permute-start | bytes 3080 | tf_op jit(solution)/shard_map/ppermute | solution.py:22
  169.6 28.4 %collective-permute-start.26 = (f32[2,8,16,1]{3,2,1,0:T(8,128)}, f32[2,8,16,1]{3,2,1,0:T(8,128)}, u32[]{:S(2)}, u32[]{:S(2)}) collective-permute-start(f32[2,8,16,1]{3,2,1,0:T(8,128)} %get-tuple-element.43), channel_id=1, source_target_pairs={{0,1},{1,2},{2,3},{3,0},{4,5},{5,6},{6,7},{7,4},{8,9},{9,10},{10,1... | collective-permute-start | bytes 3080 | tf_op jit(solution)/shard_map/ppermute | solution.py:19
  171.5 27.8 %collective-permute-start.25 = (f32[2,8,1,64]{3,2,1,0:T(1,128)}, f32[2,8,1,64]{3,2,1,0:T(1,128)S(1)}, u32[]{:S(2)}, u32[]{:S(2)}) collective-permute-start(f32[2,8,1,64]{3,2,1,0:T(1,128)} %get-tuple-element.42), channel_id=1, source_target_pairs={{4,0},{8,4},{12,8},{16,12},{20,16},{24,20},{28,24},{5,1},{9,5},{13... | collective-permute-start | bytes 12296 | tf_op jit(solution)/shard_map/ppermute | solution.py:22
  172.8 34.8 %collective-permute-start.24 = (f32[2,8,1,64]{3,2,1,0:T(1,128)}, f32[2,8,1,64]{3,2,1,0:T(1,128)}, u32[]{:S(2)}, u32[]{:S(2)}) collective-permute-start(f32[2,8,1,64]{3,2,1,0:T(1,128)} %get-tuple-element.41), channel_id=1, source_target_pairs={{0,4},{4,8},{8,12},{12,16},{16,20},{20,24},{24,28},{1,5},{5,9},{9,... | collective-permute-start | bytes 12296 | tf_op jit(solution)/shard_map/ppermute | solution.py:19
  187.8 24.6 %collective-permute-start.7 = (f32[2,8,32,1]{2,1,3,0:T(8,128)}, f32[2,8,32,1]{2,1,3,0:T(8,128)S(1)}, u32[]{:S(2)}, u32[]{:S(2)}) collective-permute-start(f32[2,8,32,1]{2,1,3,0:T(8,128)} %get-tuple-element.16), channel_id=1, source_target_pairs={{1,0},{2,1},{3,2},{0,3},{5,4},{6,5},{7,6},{4,7},{9,8},{10,9},{11,1... | collective-permute-start | bytes 6152 | tf_op jit(solution)/shard_map/ppermute | solution.py:22
  216.8 32.0 %collective-permute-start.11 = (f32[2,8,32,1]{2,1,3,0:T(8,128)}, f32[2,8,32,1]{2,1,3,0:T(8,128)S(1)}, u32[]{:S(2)}, u32[]{:S(2)}) collective-permute-start(f32[2,8,32,1]{2,1,3,0:T(8,128)} %get-tuple-element.12), channel_id=1, source_target_pairs={{1,0},{2,1},{3,2},{0,3},{5,4},{6,5},{7,6},{4,7},{9,8},{10,9},{11,1... | collective-permute-start | bytes 6152 | tf_op jit(solution)/shard_map/ppermute | solution.py:22
  222.0 36.3 %collective-permute-start.10 = (f32[2,8,32,1]{2,1,3,0:T(8,128)}, f32[2,8,32,1]{2,1,3,0:T(8,128)}, u32[]{:S(2)}, u32[]{:S(2)}) collective-permute-start(f32[2,8,32,1]{2,1,3,0:T(8,128)} %get-tuple-element.11), channel_id=1, source_target_pairs={{0,1},{1,2},{2,3},{3,0},{4,5},{5,6},{6,7},{7,4},{8,9},{9,10},{10,1... | collective-permute-start | bytes 6152 | tf_op jit(solution)/shard_map/ppermute | solution.py:19
  237.7 33.2 %collective-permute-start.31 = (f32[2,8,16,1]{3,2,1,0:T(8,128)}, f32[2,8,16,1]{3,2,1,0:T(8,128)}, u32[]{:S(2)}, u32[]{:S(2)}) collective-permute-start(f32[2,8,16,1]{3,2,1,0:T(8,128)} %get-tuple-element.40), channel_id=1, source_target_pairs={{1,0},{2,1},{3,2},{0,3},{5,4},{6,5},{7,6},{4,7},{9,8},{10,9},{11,1... | collective-permute-start | bytes 3080 | tf_op jit(solution)/shard_map/ppermute | solution.py:22
  242.9 30.0 %collective-permute-start.30 = (f32[2,8,16,1]{3,2,1,0:T(8,128)S(1)}, f32[2,8,16,1]{3,2,1,0:T(8,128)}, u32[]{:S(2)}, u32[]{:S(2)}) collective-permute-start(f32[2,8,16,1]{3,2,1,0:T(8,128)S(1)} %get-tuple-element.39), channel_id=1, source_target_pairs={{0,1},{1,2},{2,3},{3,0},{4,5},{5,6},{6,7},{7,4},{8,9},{9,10},{10,1... | collective-permute-start | bytes 3080 | tf_op jit(solution)/shard_map/ppermute | solution.py:19
  246.2 27.9 %collective-permute-start.29 = (f32[2,8,1,64]{3,2,1,0:T(1,128)}, f32[2,8,1,64]{3,2,1,0:T(1,128)S(1)}, u32[]{:S(2)}, u32[]{:S(2)}) collective-permute-start(f32[2,8,1,64]{3,2,1,0:T(1,128)} %get-tuple-element.38), channel_id=1, source_target_pairs={{4,0},{8,4},{12,8},{16,12},{20,16},{24,20},{28,24},{5,1},{9,5},{13... | collective-permute-start | bytes 12296 | tf_op jit(solution)/shard_map/ppermute | solution.py:22
  248.9 34.1 %collective-permute-start.28 = (f32[2,8,1,64]{3,2,1,0:T(1,128)}, f32[2,8,1,64]{3,2,1,0:T(1,128)}, u32[]{:S(2)}, u32[]{:S(2)}) collective-permute-start(f32[2,8,1,64]{3,2,1,0:T(1,128)} %get-tuple-element.37), channel_id=1, source_target_pairs={{0,4},{4,8},{8,12},{12,16},{16,20},{20,24},{24,28},{1,5},{5,9},{9,... | collective-permute-start | bytes 12296 | tf_op jit(solution)/shard_map/ppermute | solution.py:19
  262.7 25.8 %collective-permute-start.15 = (f32[2,8,32,1]{2,1,3,0:T(8,128)}, f32[2,8,32,1]{2,1,3,0:T(8,128)S(1)}, u32[]{:S(2)}, u32[]{:S(2)}) collective-permute-start(f32[2,8,32,1]{2,1,3,0:T(8,128)} %get-tuple-element.8), channel_id=1, source_target_pairs={{1,0},{2,1},{3,2},{0,3},{5,4},{6,5},{7,6},{4,7},{9,8},{10,9},{11,1... | collective-permute-start | bytes 6152 | tf_op jit(solution)/shard_map/ppermute | solution.py:22
  (33 other events, 485.9 us)
Sparse Core Ops, SparseCore 0:
  294.8 131.5 all-reduce.1
where the time goes:
time: 437 us; the launch traced here: 435 us
  starting transfers between devices  205 us (47%)
  waiting for transfers between devices  132 us (30%)
  local copies, waits for them, and re-layouts  54.8 us (13%)
  other arithmetic  29 us (7%)
  between operations  14.2 us (3%)
    psum x1, waiting for transfers between devices, body(): summed = lax.psum(partial_value, 'mem')  132 us
    ppermute x24, starting transfers between devices, with_halo(): lax.ppermute(lax.slice_in_dim(block, block.shape[dim] - width, None, axis...  130 us
    ppermute x24, starting transfers between devices, with_halo(): lax.ppermute(lax.slice_in_dim(block, 0, width, axis=dim), axis, backward)  74.5 us
    slice x28, local copies, waits for them, and re-layouts, with_halo(): lax.slice_in_dim(block, block.shape[dim] - width, None, axis=dim)  19.6 us
    div x11, other arithmetic, diffuse_single(): smoothed = (source + stiffness * beside_all) / (1.0 + 4.0 * stiffness)  14.9 us
    reduce_sum x2, other arithmetic, coarsen(): return jnp.mean(blocks, axis=(-3, -1))  9.21 us
  transfers between devices with their start and end apart: 49, of which 1 were waited for; matrix products, arithmetic and copies ran while one was open for 13% of the time, Pallas kernels for 0%

commit v1 on v0

--- a/solution.py
+++ b/solution.py
@@ -61,7 +61,11 @@
         running = running + weight * member_field * refine(coarse, factor)
     partial_value = jnp.sum(running, axis=0)
     member_count = members.shape[0] * lax.axis_size("mem")
-    summed = lax.psum(partial_value, "mem")
+    peers = lax.axis_size("mem")
+    summed, far = (partial_value, 1)
+    while far < peers:
+        summed = summed + lax.ppermute(summed, "mem", [(i_2, i_2 ^ far) for i_2 in range(peers)])
+        far = 2 * far
     return summed / (member_count - 1)
 
 

time: 437 us -> 384 us (0.88); the launches traced: 435 us -> 376 us
  waiting for transfers between devices: 132 us -> 59 us
  starting transfers between devices: 205 us -> 236 us
  between operations: 14.2 us -> 0.91 us
    psum x1 -> x0, waiting for transfers between devices: 132 us -> none  [body(): summed = lax.psum(partial_value, 'mem')]
    ppermute x0 -> x4, waiting for transfers between devices: none -> 58.9 us  [body(): lax.ppermute(summed, 'mem', [(i_2, i_2 ^ far) for i_2 in range(peers)])]
    ppermute x0 -> x4, starting transfers between devices: none -> 31 us  [body(): lax.ppermute(summed, 'mem', [(i_2, i_2 ^ far) for i_2 in range(peers)])]
  transfers between devices with their start and end apart: 49 -> 52, of which waited for: 1 -> 4; matrix products, arithmetic and copies ran while one was open for 13% -> 15% of each run, Pallas kernels for 0% -> 0%
where the time goes in v1:
time: 384 us; the launch traced here: 376 us
  starting transfers between devices  236 us (61%)
  waiting for transfers between devices  59 us (15%)
  local copies, waits for them, and re-layouts  53.6 us (14%)
  other arithmetic  27 us (7%)
    ppermute x24, starting transfers between devices, with_halo(): lax.ppermute(lax.slice_in_dim(block, block.shape[dim] - width, None, axis...  130 us
    ppermute x24, starting transfers between devices, with_halo(): lax.ppermute(lax.slice_in_dim(block, 0, width, axis=dim), axis, backward)  74.5 us
    ppermute x4, waiting for transfers between devices, body(): lax.ppermute(summed, 'mem', [(i_2, i_2 ^ far) for i_2 in range(peers)])  58.9 us
    ppermute x4, starting transfers between devices, body(): lax.ppermute(summed, 'mem', [(i_2, i_2 ^ far) for i_2 in range(peers)])  31 us
    slice x28, local copies, waits for them, and re-layouts, with_halo(): lax.slice_in_dim(block, block.shape[dim] - width, None, axis=dim)  19.5 us
    div x11, other arithmetic, diffuse_single(): smoothed = (source + stiffness * beside_all) / (1.0 + 4.0 * stiffness)  15 us
    reduce_sum x2, other arithmetic, coarsen(): return jnp.mean(blocks, axis=(-3, -1))  9.21 us
    slice x4, local copies, waits for them, and re-layouts, with_halo(): lax.slice_in_dim(block, 0, width, axis=dim)  8.6 us
  transfers between devices with their start and end apart: 52, of which 4 were waited for; matrix products, arithmetic and copies ran while one was open for 15% of the time, Pallas kernels for 0%

profile of v1, /device:TPU:1, one launch (start us, length us, event | category | flops | bytes accessed | tf_op | source)
XLA Modules:
  0.0 376.3 jit_solution(9936508689801043121)
XLA Ops:
  6.8 5.6 %reduce_sum.27 = f32[2,8,16,64]{1,3,2,0:T(8,128)S(1)} reduce(f32[2,8,16,2,64,2]{1,5,4,3,2,0:T(2,128)} %bitcast.6, f32[]{:T(128)} %constant.30.clone.1), dimensions={3,5}, to_apply=%region_0.0 | reduce | flops 49152 | bytes 327684 | tf_op jit(solution)/shard_map/reduce_sum | solution.py:34
  13.6 8.4 %collective-permute-start.19 = (f32[2,8,16,1]{3,2,1,0:T(8,128)}, f32[2,8,16,1]{3,2,1,0:T(8,128)}, u32[]{:S(2)}, u32[]{:S(2)}) collective-permute-start(f32[2,8,16,1]{3,2,1,0:T(8,128)} %get-tuple-element.52), channel_id=1, source_target_pairs={{1,0},{2,1},{3,2},{0,3},{5,4},{6,5},{7,6},{4,7},{9,8},{10,9},{11,1... | collective-permute-start | bytes 3080 | tf_op jit(solution)/shard_map/ppermute | solution.py:22
  32.2 8.6 %collective-permute-start.32 = (f32[2,8,1,32]{1,3,2,0:T(8,128)S(1)}, f32[2,8,1,32]{1,3,2,0:T(8,128)S(1)}, u32[]{:S(2)}, u32[]{:S(2)}) collective-permute-start(f32[2,8,1,32]{1,3,2,0:T(8,128)S(1)} %get-tuple-element.33), channel_id=1, source_target_pairs={{0,4},{4,8},{8,12},{12,16},{16,20},{20,24},{24,28},{1,5},{5,9},{9,... | collective-permute-start | bytes 6152 | tf_op jit(solution)/shard_map/ppermute | solution.py:19
  52.3 9.4 %collective-permute-start.36 = (f32[2,8,1,32]{1,3,2,0:T(8,128)}, f32[2,8,1,32]{1,3,2,0:T(8,128)}, u32[]{:S(2)}, u32[]{:S(2)}) collective-permute-start(f32[2,8,1,32]{1,3,2,0:T(8,128)} %get-tuple-element.29), channel_id=1, source_target_pairs={{0,4},{4,8},{8,12},{12,16},{16,20},{20,24},{24,28},{1,5},{5,9},{9,... | collective-permute-start | bytes 6152 | tf_op jit(solution)/shard_map/ppermute | solution.py:19
  68.1 8.2 %collective-permute-start.16 = (f32[2,8,1,64]{3,2,1,0:T(1,128)}, f32[2,8,1,64]{3,2,1,0:T(1,128)S(1)}, u32[]{:S(2)}, u32[]{:S(2)}) collective-permute-start(f32[2,8,1,64]{3,2,1,0:T(1,128)} %get-tuple-element.49), channel_id=1, source_target_pairs={{0,4},{4,8},{8,12},{12,16},{16,20},{20,24},{24,28},{1,5},{5,9},{9,... | collective-permute-start | bytes 12296 | tf_op jit(solution)/shard_map/ppermute | solution.py:19
  76.3 5.2 %collective-permute-start.3 = (f32[2,8,32,1]{2,1,3,0:T(8,128)}, f32[2,8,32,1]{2,1,3,0:T(8,128)S(1)}, u32[]{:S(2)}, u32[]{:S(2)}) collective-permute-start(f32[2,8,32,1]{2,1,3,0:T(8,128)} %get-tuple-element.20), channel_id=1, source_target_pairs={{1,0},{2,1},{3,2},{0,3},{5,4},{6,5},{7,6},{4,7},{9,8},{10,9},{11,1... | collective-permute-start | bytes 6152 | tf_op jit(solution)/shard_map/ppermute | solution.py:22
  91.3 8.8 %collective-permute-start.40 = (f32[2,8,1,32]{1,3,2,0:T(8,128)S(1)}, f32[2,8,1,32]{1,3,2,0:T(8,128)S(1)}, u32[]{:S(2)}, u32[]{:S(2)}) collective-permute-start(f32[2,8,1,32]{1,3,2,0:T(8,128)S(1)} %get-tuple-element.25), channel_id=1, source_target_pairs={{0,4},{4,8},{8,12},{12,16},{16,20},{20,24},{24,28},{1,5},{5,9},{9,... | collective-permute-start | bytes 6152 | tf_op jit(solution)/shard_map/ppermute | solution.py:19
  100.1 5.2 %collective-permute-start.23 = (f32[2,8,16,1]{3,2,1,0:T(8,128)S(1)}, f32[2,8,16,1]{3,2,1,0:T(8,128)S(1)}, u32[]{:S(2)}, u32[]{:S(2)}) collective-permute-start(f32[2,8,16,1]{3,2,1,0:T(8,128)S(1)} %get-tuple-element.48), channel_id=1, source_target_pairs={{1,0},{2,1},{3,2},{0,3},{5,4},{6,5},{7,6},{4,7},{9,8},{10,9},{11,1... | collective-permute-start | bytes 3080 | tf_op jit(solution)/shard_map/ppermute | solution.py:22
  108.6 8.8 %collective-permute-start.20 = (f32[2,8,1,64]{3,2,1,0:T(1,128)S(1)}, f32[2,8,1,64]{3,2,1,0:T(1,128)S(1)}, u32[]{:S(2)}, u32[]{:S(2)}) collective-permute-start(f32[2,8,1,64]{3,2,1,0:T(1,128)S(1)} %get-tuple-element.45), channel_id=1, source_target_pairs={{0,4},{4,8},{8,12},{12,16},{16,20},{20,24},{24,28},{1,5},{5,9},{9,... | collective-permute-start | bytes 12296 | tf_op jit(solution)/shard_map/ppermute | solution.py:19
  122.0 8.8 %collective-permute-start = (f32[2,8,1,128]{3,1,2,0:T(8,128)S(1)}, f32[2,8,1,128]{3,1,2,0:T(8,128)S(1)}, u32[]{:S(2)}, u32[]{:S(2)}) collective-permute-start(f32[2,8,1,128]{3,1,2,0:T(8,128)S(1)} %copy.348), channel_id=1, source_target_pairs={{0,4},{4,8},{8,12},{12,16},{16,20},{20,24},{24,28},{1,5},{5,9},{9,... | collective-permute-start | bytes 24584 | tf_op jit(solution)/shard_map/ppermute | solution.py:19
  130.9 5.2 %collective-permute-start.47 = (f32[2,8,8,1]{1,3,2,0:T(1,128)}, f32[2,8,8,1]{1,3,2,0:T(1,128)}, u32[]{:S(2)}, u32[]{:S(2)}) collective-permute-start(f32[2,8,8,1]{1,3,2,0:T(1,128)} %get-tuple-element.24), channel_id=1, source_target_pairs={{1,0},{2,1},{3,2},{0,3},{5,4},{6,5},{7,6},{4,7},{9,8},{10,9},{11,1... | collective-permute-start | bytes 1544 | tf_op jit(solution)/shard_map/ppermute | solution.py:22
  143.0 8.8 %collective-permute-start.44 = (f32[2,8,1,32]{1,3,2,0:T(8,128)}, f32[2,8,1,32]{1,3,2,0:T(8,128)S(1)}, u32[]{:S(2)}, u32[]{:S(2)}) collective-permute-start(f32[2,8,1,32]{1,3,2,0:T(8,128)} %get-tuple-element.21), channel_id=1, source_target_pairs={{0,4},{4,8},{8,12},{12,16},{16,20},{20,24},{24,28},{1,5},{5,9},{9,... | collective-permute-start | bytes 6152 | tf_op jit(solution)/shard_map/ppermute | solution.py:19
  152.4 5.3 %collective-permute-start.27 = (f32[2,8,16,1]{3,2,1,0:T(8,128)}, f32[2,8,16,1]{3,2,1,0:T(8,128)}, u32[]{:S(2)}, u32[]{:S(2)}) collective-permute-start(f32[2,8,16,1]{3,2,1,0:T(8,128)} %get-tuple-element.44), channel_id=1, source_target_pairs={{1,0},{2,1},{3,2},{0,3},{5,4},{6,5},{7,6},{4,7},{9,8},{10,9},{11,1... | collective-permute-start | bytes 3080 | tf_op jit(solution)/shard_map/ppermute | solution.py:22
  166.2 9.4 %collective-permute-start.24 = (f32[2,8,1,64]{3,2,1,0:T(1,128)}, f32[2,8,1,64]{3,2,1,0:T(1,128)}, u32[]{:S(2)}, u32[]{:S(2)}) collective-permute-start(f32[2,8,1,64]{3,2,1,0:T(1,128)} %get-tuple-element.41), channel_id=1, source_target_pairs={{0,4},{4,8},{8,12},{12,16},{16,20},{20,24},{24,28},{1,5},{5,9},{9,... | collective-permute-start | bytes 12296 | tf_op jit(solution)/shard_map/ppermute | solution.py:19
  192.8 8.2 %collective-permute-start.4 = (f32[2,8,1,128]{3,1,2,0:T(8,128)}, f32[2,8,1,128]{3,1,2,0:T(8,128)S(1)}, u32[]{:S(2)}, u32[]{:S(2)}) collective-permute-start(f32[2,8,1,128]{3,1,2,0:T(8,128)} %copy.352), channel_id=1, source_target_pairs={{0,4},{4,8},{8,12},{12,16},{16,20},{20,24},{24,28},{1,5},{5,9},{9,... | collective-permute-start | bytes 24584 | tf_op jit(solution)/shard_map/ppermute | solution.py:19
  221.7 8.8 %collective-permute-start.8 = (f32[2,8,1,128]{3,1,2,0:T(8,128)}, f32[2,8,1,128]{3,1,2,0:T(8,128)S(1)}, u32[]{:S(2)}, u32[]{:S(2)}) collective-permute-start(f32[2,8,1,128]{3,1,2,0:T(8,128)} %copy.356), channel_id=1, source_target_pairs={{0,4},{4,8},{8,12},{12,16},{16,20},{20,24},{24,28},{1,5},{5,9},{9,... | collective-permute-start | bytes 24584 | tf_op jit(solution)/shard_map/ppermute | solution.py:19
  231.1 5.1 %collective-permute-start.31 = (f32[2,8,16,1]{3,2,1,0:T(8,128)}, f32[2,8,16,1]{3,2,1,0:T(8,128)}, u32[]{:S(2)}, u32[]{:S(2)}) collective-permute-start(f32[2,8,16,1]{3,2,1,0:T(8,128)} %get-tuple-element.40), channel_id=1, source_target_pairs={{1,0},{2,1},{3,2},{0,3},{5,4},{6,5},{7,6},{4,7},{9,8},{10,9},{11,1... | collective-permute-start | bytes 3080 | tf_op jit(solution)/shard_map/ppermute | solution.py:22
  242.3 9.4 %collective-permute-start.28 = (f32[2,8,1,64]{3,2,1,0:T(1,128)}, f32[2,8,1,64]{3,2,1,0:T(1,128)}, u32[]{:S(2)}, u32[]{:S(2)}) collective-permute-start(f32[2,8,1,64]{3,2,1,0:T(1,128)} %get-tuple-element.37), channel_id=1, source_target_pairs={{0,4},{4,8},{8,12},{12,16},{16,20},{20,24},{24,28},{1,5},{5,9},{9,... | collective-permute-start | bytes 12296 | tf_op jit(solution)/shard_map/ppermute | solution.py:19
  267.5 8.8 %collective-permute-start.12 = (f32[2,8,1,128]{3,1,2,0:T(8,128)}, f32[2,8,1,128]{3,1,2,0:T(8,128)}, u32[]{:S(2)}, u32[]{:S(2)}) collective-permute-start(f32[2,8,1,128]{3,1,2,0:T(8,128)} %copy.360), channel_id=1, source_target_pairs={{0,4},{4,8},{8,12},{12,16},{16,20},{20,24},{24,28},{1,5},{5,9},{9,... | collective-permute-start | bytes 24584 | tf_op jit(solution)/shard_map/ppermute | solution.py:19
  285.4 15.2 %collective-permute-start.48 = (f32[8,32,128]{1,0,2:T(8,128)S(1)}, f32[8,32,128]{1,0,2:T(8,128)S(1)}, u32[]{:S(2)}, u32[]{:S(2)}) collective-permute-start(f32[8,32,128]{1,0,2:T(8,128)S(1)} %fusion.3), channel_id=1, source_target_pairs={{0,32},{32,0},{64,96},{96,64},{128,160},{160,128},{192,224},{224,1... | collective-permute-start | bytes 393224 | tf_op jit(solution)/shard_map/ppermute | solution.py:67
  305.4 11.8 %collective-permute-done.49 = f32[8,32,128]{1,0,2:T(8,128)S(1)} collective-permute-done((f32[8,32,128]{1,0,2:T(8,128)S(1)}, f32[8,32,128]{1,0,2:T(8,128)S(1)}, u32[]{:S(2)}, u32[]{:S(2)}) %collective-permute-start.49) | collective-permute-done | bytes 131104 | tf_op jit(solution)/shard_map/ppermute | solution.py:67
  321.4 22.6 %collective-permute-done.50 = f32[8,32,128]{1,0,2:T(8,128)S(1)} collective-permute-done((f32[8,32,128]{1,0,2:T(8,128)S(1)}, f32[8,32,128]{1,0,2:T(8,128)S(1)}, u32[]{:S(2)}, u32[]{:S(2)}) %collective-permute-start.50) | collective-permute-done | bytes 131104 | tf_op jit(solution)/shard_map/ppermute | solution.py:67
  344.1 8.4 %collective-permute-start.51 = (f32[8,32,128]{1,0,2:T(8,128)S(1)}, f32[8,32,128]{1,0,2:T(8,128)S(1)}, u32[]{:S(2)}, u32[]{:S(2)}) collective-permute-start(f32[8,32,128]{1,0,2:T(8,128)S(1)} %add.214), channel_id=1, source_target_pairs={{0,256},{32,288},{64,320},{96,352},{128,384},{160,416},{192,448},{... | collective-permute-start | bytes 393224 | tf_op jit(solution)/shard_map/ppermute | solution.py:67
  352.5 22.9 %collective-permute-done.51 = f32[8,32,128]{1,0,2:T(8,128)S(1)} collective-permute-done((f32[8,32,128]{1,0,2:T(8,128)S(1)}, f32[8,32,128]{1,0,2:T(8,128)S(1)}, u32[]{:S(2)}, u32[]{:S(2)}) %collective-permute-start.51) | collective-permute-done | bytes 131104 | tf_op jit(solution)/shard_map/ppermute | solution.py:67
  (170 shorter events, 148.6 us)
Async XLA Ops:
  13.6 69.4 %collective-permute-start.19 = (f32[2,8,16,1]{3,2,1,0:T(8,128)}, f32[2,8,16,1]{3,2,1,0:T(8,128)}, u32[]{:S(2)}, u32[]{:S(2)}) collective-permute-start(f32[2,8,16,1]{3,2,1,0:T(8,128)} %get-tuple-element.52), channel_id=1, source_target_pairs={{1,0},{2,1},{3,2},{0,3},{5,4},{6,5},{7,6},{4,7},{9,8},{10,9},{11,1... | collective-permute-start | bytes 3080 | tf_op jit(solution)/shard_map/ppermute | solution.py:22
  45.1 19.7 %collective-permute-start.39 = (f32[2,8,8,1]{1,3,2,0:T(1,128)}, f32[2,8,8,1]{1,3,2,0:T(1,128)S(1)}, u32[]{:S(2)}, u32[]{:S(2)}) collective-permute-start(f32[2,8,8,1]{1,3,2,0:T(1,128)} %get-tuple-element.32), channel_id=1, source_target_pairs={{1,0},{2,1},{3,2},{0,3},{5,4},{6,5},{7,6},{4,7},{9,8},{10,9},{11,1... | collective-permute-start | bytes 1544 | tf_op jit(solution)/shard_map/ppermute | solution.py:22
  52.3 24.0 %collective-permute-start.36 = (f32[2,8,1,32]{1,3,2,0:T(8,128)}, f32[2,8,1,32]{1,3,2,0:T(8,128)}, u32[]{:S(2)}, u32[]{:S(2)}) collective-permute-start(f32[2,8,1,32]{1,3,2,0:T(8,128)} %get-tuple-element.29), channel_id=1, source_target_pairs={{0,4},{4,8},{8,12},{12,16},{16,20},{20,24},{24,28},{1,5},{5,9},{9,... | collective-permute-start | bytes 6152 | tf_op jit(solution)/shard_map/ppermute | solution.py:19
  76.3 66.6 %collective-permute-start.3 = (f32[2,8,32,1]{2,1,3,0:T(8,128)}, f32[2,8,32,1]{2,1,3,0:T(8,128)S(1)}, u32[]{:S(2)}, u32[]{:S(2)}) collective-permute-start(f32[2,8,32,1]{2,1,3,0:T(8,128)} %get-tuple-element.20), channel_id=1, source_target_pairs={{1,0},{2,1},{3,2},{0,3},{5,4},{6,5},{7,6},{4,7},{9,8},{10,9},{11,1... | collective-permute-start | bytes 6152 | tf_op jit(solution)/shard_map/ppermute | solution.py:22
  108.6 22.3 %collective-permute-start.20 = (f32[2,8,1,64]{3,2,1,0:T(1,128)S(1)}, f32[2,8,1,64]{3,2,1,0:T(1,128)S(1)}, u32[]{:S(2)}, u32[]{:S(2)}) collective-permute-start(f32[2,8,1,64]{3,2,1,0:T(1,128)S(1)} %get-tuple-element.45), channel_id=1, source_target_pairs={{0,4},{4,8},{8,12},{12,16},{16,20},{20,24},{24,28},{1,5},{5,9},{9,... | collective-permute-start | bytes 12296 | tf_op jit(solution)/shard_map/ppermute | solution.py:19
  118.8 32.9 %collective-permute-start.2 = (f32[2,8,32,1]{2,1,3,0:T(8,128)}, f32[2,8,32,1]{2,1,3,0:T(8,128)S(1)}, u32[]{:S(2)}, u32[]{:S(2)}) collective-permute-start(f32[2,8,32,1]{2,1,3,0:T(8,128)} %get-tuple-element.19), channel_id=1, source_target_pairs={{0,1},{1,2},{2,3},{3,0},{4,5},{5,6},{6,7},{7,4},{8,9},{9,10},{10,1... | collective-permute-start | bytes 6152 | tf_op jit(solution)/shard_map/ppermute | solution.py:19
  130.9 32.1 %collective-permute-start.47 = (f32[2,8,8,1]{1,3,2,0:T(1,128)}, f32[2,8,8,1]{1,3,2,0:T(1,128)}, u32[]{:S(2)}, u32[]{:S(2)}) collective-permute-start(f32[2,8,8,1]{1,3,2,0:T(1,128)} %get-tuple-element.24), channel_id=1, source_target_pairs={{1,0},{2,1},{3,2},{0,3},{5,4},{6,5},{7,6},{4,7},{9,8},{10,9},{11,1... | collective-permute-start | bytes 1544 | tf_op jit(solution)/shard_map/ppermute | solution.py:22
  137.0 27.9 %collective-permute-start.46 = (f32[2,8,8,1]{1,3,2,0:T(1,128)}, f32[2,8,8,1]{1,3,2,0:T(1,128)}, u32[]{:S(2)}, u32[]{:S(2)}) collective-permute-start(f32[2,8,8,1]{1,3,2,0:T(1,128)} %get-tuple-element.23), channel_id=1, source_target_pairs={{0,1},{1,2},{2,3},{3,0},{4,5},{5,6},{6,7},{7,4},{8,9},{9,10},{10,1... | collective-permute-start | bytes 1544 | tf_op jit(solution)/shard_map/ppermute | solution.py:19
  140.3 25.9 %collective-permute-start.45 = (f32[2,8,1,32]{1,3,2,0:T(8,128)}, f32[2,8,1,32]{1,3,2,0:T(8,128)}, u32[]{:S(2)}, u32[]{:S(2)}) collective-permute-start(f32[2,8,1,32]{1,3,2,0:T(8,128)} %get-tuple-element.22), channel_id=1, source_target_pairs={{4,0},{8,4},{12,8},{16,12},{20,16},{24,20},{28,24},{5,1},{9,5},{13... | collective-permute-start | bytes 6152 | tf_op jit(solution)/shard_map/ppermute | solution.py:22
  143.0 32.7 %collective-permute-start.44 = (f32[2,8,1,32]{1,3,2,0:T(8,128)}, f32[2,8,1,32]{1,3,2,0:T(8,128)S(1)}, u32[]{:S(2)}, u32[]{:S(2)}) collective-permute-start(f32[2,8,1,32]{1,3,2,0:T(8,128)} %get-tuple-element.21), channel_id=1, source_target_pairs={{0,4},{4,8},{8,12},{12,16},{16,20},{20,24},{24,28},{1,5},{5,9},{9,... | collective-permute-start | bytes 6152 | tf_op jit(solution)/shard_map/ppermute | solution.py:19
  152.4 37.2 %collective-permute-start.27 = (f32[2,8,16,1]{3,2,1,0:T(8,128)}, f32[2,8,16,1]{3,2,1,0:T(8,128)}, u32[]{:S(2)}, u32[]{:S(2)}) collective-permute-start(f32[2,8,16,1]{3,2,1,0:T(8,128)} %get-tuple-element.44), channel_id=1, source_target_pairs={{1,0},{2,1},{3,2},{0,3},{5,4},{6,5},{7,6},{4,7},{9,8},{10,9},{11,1... | collective-permute-start | bytes 3080 | tf_op jit(solution)/shard_map/ppermute | solution.py:22
  163.0 28.5 %collective-permute-start.26 = (f32[2,8,16,1]{3,2,1,0:T(8,128)}, f32[2,8,16,1]{3,2,1,0:T(8,128)}, u32[]{:S(2)}, u32[]{:S(2)}) collective-permute-start(f32[2,8,16,1]{3,2,1,0:T(8,128)} %get-tuple-element.43), channel_id=1, source_target_pairs={{0,1},{1,2},{2,3},{3,0},{4,5},{5,6},{6,7},{7,4},{8,9},{9,10},{10,1... | collective-permute-start | bytes 3080 | tf_op jit(solution)/shard_map/ppermute | solution.py:19
  164.9 27.8 %collective-permute-start.25 = (f32[2,8,1,64]{3,2,1,0:T(1,128)}, f32[2,8,1,64]{3,2,1,0:T(1,128)S(1)}, u32[]{:S(2)}, u32[]{:S(2)}) collective-permute-start(f32[2,8,1,64]{3,2,1,0:T(1,128)} %get-tuple-element.42), channel_id=1, source_target_pairs={{4,0},{8,4},{12,8},{16,12},{20,16},{24,20},{28,24},{5,1},{9,5},{13... | collective-permute-start | bytes 12296 | tf_op jit(solution)/shard_map/ppermute | solution.py:22
  166.2 34.8 %collective-permute-start.24 = (f32[2,8,1,64]{3,2,1,0:T(1,128)}, f32[2,8,1,64]{3,2,1,0:T(1,128)}, u32[]{:S(2)}, u32[]{:S(2)}) collective-permute-start(f32[2,8,1,64]{3,2,1,0:T(1,128)} %get-tuple-element.41), channel_id=1, source_target_pairs={{0,4},{4,8},{8,12},{12,16},{16,20},{20,24},{24,28},{1,5},{5,9},{9,... | collective-permute-start | bytes 12296 | tf_op jit(solution)/shard_map/ppermute | solution.py:19
  181.3 24.6 %collective-permute-start.7 = (f32[2,8,32,1]{2,1,3,0:T(8,128)}, f32[2,8,32,1]{2,1,3,0:T(8,128)S(1)}, u32[]{:S(2)}, u32[]{:S(2)}) collective-permute-start(f32[2,8,32,1]{2,1,3,0:T(8,128)} %get-tuple-element.16), channel_id=1, source_target_pairs={{1,0},{2,1},{3,2},{0,3},{5,4},{6,5},{7,6},{4,7},{9,8},{10,9},{11,1... | collective-permute-start | bytes 6152 | tf_op jit(solution)/shard_map/ppermute | solution.py:22
  210.3 32.0 %collective-permute-start.11 = (f32[2,8,32,1]{2,1,3,0:T(8,128)}, f32[2,8,32,1]{2,1,3,0:T(8,128)S(1)}, u32[]{:S(2)}, u32[]{:S(2)}) collective-permute-start(f32[2,8,32,1]{2,1,3,0:T(8,128)} %get-tuple-element.12), channel_id=1, source_target_pairs={{1,0},{2,1},{3,2},{0,3},{5,4},{6,5},{7,6},{4,7},{9,8},{10,9},{11,1... | collective-permute-start | bytes 6152 | tf_op jit(solution)/shard_map/ppermute | solution.py:22
  215.4 36.2 %collective-permute-start.10 = (f32[2,8,32,1]{2,1,3,0:T(8,128)}, f32[2,8,32,1]{2,1,3,0:T(8,128)}, u32[]{:S(2)}, u32[]{:S(2)}) collective-permute-start(f32[2,8,32,1]{2,1,3,0:T(8,128)} %get-tuple-element.11), channel_id=1, source_target_pairs={{0,1},{1,2},{2,3},{3,0},{4,5},{5,6},{6,7},{7,4},{8,9},{9,10},{10,1... | collective-permute-start | bytes 6152 | tf_op jit(solution)/shard_map/ppermute | solution.py:19
  231.1 33.2 %collective-permute-start.31 = (f32[2,8,16,1]{3,2,1,0:T(8,128)}, f32[2,8,16,1]{3,2,1,0:T(8,128)}, u32[]{:S(2)}, u32[]{:S(2)}) collective-permute-start(f32[2,8,16,1]{3,2,1,0:T(8,128)} %get-tuple-element.40), channel_id=1, source_target_pairs={{1,0},{2,1},{3,2},{0,3},{5,4},{6,5},{7,6},{4,7},{9,8},{10,9},{11,1... | collective-permute-start | bytes 3080 | tf_op jit(solution)/shard_map/ppermute | solution.py:22
  236.3 29.9 %collective-permute-start.30 = (f32[2,8,16,1]{3,2,1,0:T(8,128)S(1)}, f32[2,8,16,1]{3,2,1,0:T(8,128)}, u32[]{:S(2)}, u32[]{:S(2)}) collective-permute-start(f32[2,8,16,1]{3,2,1,0:T(8,128)S(1)} %get-tuple-element.39), channel_id=1, source_target_pairs={{0,1},{1,2},{2,3},{3,0},{4,5},{5,6},{6,7},{7,4},{8,9},{9,10},{10,1... | collective-permute-start | bytes 3080 | tf_op jit(solution)/shard_map/ppermute | solution.py:19
  239.6 27.9 %collective-permute-start.29 = (f32[2,8,1,64]{3,2,1,0:T(1,128)}, f32[2,8,1,64]{3,2,1,0:T(1,128)S(1)}, u32[]{:S(2)}, u32[]{:S(2)}) collective-permute-start(f32[2,8,1,64]{3,2,1,0:T(1,128)} %get-tuple-element.38), channel_id=1, source_target_pairs={{4,0},{8,4},{12,8},{16,12},{20,16},{24,20},{28,24},{5,1},{9,5},{13... | collective-permute-start | bytes 12296 | tf_op jit(solution)/shard_map/ppermute | solution.py:22
  242.3 34.1 %collective-permute-start.28 = (f32[2,8,1,64]{3,2,1,0:T(1,128)}, f32[2,8,1,64]{3,2,1,0:T(1,128)}, u32[]{:S(2)}, u32[]{:S(2)}) collective-permute-start(f32[2,8,1,64]{3,2,1,0:T(1,128)} %get-tuple-element.37), channel_id=1, source_target_pairs={{0,4},{4,8},{8,12},{12,16},{16,20},{20,24},{24,28},{1,5},{5,9},{9,... | collective-permute-start | bytes 12296 | tf_op jit(solution)/shard_map/ppermute | solution.py:19
  256.0 25.8 %collective-permute-start.15 = (f32[2,8,32,1]{2,1,3,0:T(8,128)}, f32[2,8,32,1]{2,1,3,0:T(8,128)S(1)}, u32[]{:S(2)}, u32[]{:S(2)}) collective-permute-start(f32[2,8,32,1]{2,1,3,0:T(8,128)} %get-tuple-element.8), channel_id=1, source_target_pairs={{1,0},{2,1},{3,2},{0,3},{5,4},{6,5},{7,6},{4,7},{9,8},{10,9},{11,1... | collective-permute-start | bytes 6152 | tf_op jit(solution)/shard_map/ppermute | solution.py:22
  317.2 26.9 %collective-permute-start.50 = (f32[8,32,128]{1,0,2:T(8,128)S(1)}, f32[8,32,128]{1,0,2:T(8,128)S(1)}, u32[]{:S(2)}, u32[]{:S(2)}) collective-permute-start(f32[8,32,128]{1,0,2:T(8,128)S(1)} %add.213), channel_id=1, source_target_pairs={{0,128},{32,160},{64,192},{96,224},{128,0},{160,32},{192,64},{224,... | collective-permute-start | bytes 393224 | tf_op jit(solution)/shard_map/ppermute | solution.py:67
  344.1 31.3 %collective-permute-start.51 = (f32[8,32,128]{1,0,2:T(8,128)S(1)}, f32[8,32,128]{1,0,2:T(8,128)S(1)}, u32[]{:S(2)}, u32[]{:S(2)}) collective-permute-start(f32[8,32,128]{1,0,2:T(8,128)S(1)} %add.214), channel_id=1, source_target_pairs={{0,256},{32,288},{64,320},{96,352},{128,384},{160,416},{192,448},{... | collective-permute-start | bytes 393224 | tf_op jit(solution)/shard_map/ppermute | solution.py:67
  (36 other events, 536.1 us)
